TPU v7x, 256 devices: a whole 4x4x8 slice. The times are simulated.
256 devices in a mesh: neur: 32 (over y, z_hi, core), tm: 8 (over x, z_lo).
Axes of the slice: x: 4, y: 4, z: 8 (z_hi: 4, z_lo: 2; z = z_hi * 2 + z_lo), core: 2. Of those that a mesh axis runs over, the one named last changes fastest.
Arguments:
- spikes: int32 [1024, 262144], P(None, ('neur', 'tm')), may hold values from 0 to 9
- held_in: int32 [262144], P(('neur', 'tm')), may hold values 0 or 1
- readin_weight: bfloat16 [262144, 1024], P(('neur', 'tm')), may hold values from -0.01171875 to 0.01171875
- qkv_weight: bfloat16 [1024, 3, 1024], P(None, None, 'tm'), may hold values from -0.1875 to 0.1875
- out_weight: bfloat16 [1024, 1024], P('tm'), may hold values from -0.1875 to 0.1875
- up_weight: bfloat16 [1024, 4096], P(None, 'tm'), may hold values from -0.1875 to 0.1875
- down_weight: bfloat16 [4096, 1024], P('tm'), may hold values from -0.09375 to 0.09375
- norm_gain: float32 [1024], replicated, may hold values from 0.25 to 1.75
- mlp_gain: float32 [1024], replicated, may hold values from 0.25 to 1.75
- final_gain: float32 [1024], replicated, may hold values from 0.25 to 1.75
- readout_weight: bfloat16 [262144, 1024], P(('neur', 'tm')), may hold values from -0.1875 to 0.1875
- readout_bias: float32 [262144], P(('neur', 'tm')), may hold values from -3 to 3
Outputs:
- latents: bfloat16 [1024, 1024], P('neur')
- neuron_bits: float32 [262144], P(('neur', 'tm'))
- bits_per_spike: float32 [], replicated
All inputs are finite; a program needn't handle non-finite values. No bound on the sum of `held_in` on one device may be relied on, other than what follows from the above.
Results may differ from a plain program's by a relative error of at most 0.006.
Values may be sent and summed in bfloat16 or wider, within the bound.
No kernel may reach another device: no remote copies, remote signals or barrier semaphores. Data moves between devices by JAX's collectives and lax.ppermute only.
A program may use at most 64 MiB of HBM per device.

v0:
```python
import math
import jax
import jax.numpy as jnp
from jax import lax
from jax.sharding import PartitionSpec as P

HEAD_DIM = 128


def normed(values, gain_vec):
    return values * lax.rsqrt(jnp.mean(values * values, -1, keepdims=True) + 1e-05) * gain_vec


def on_device(
    spikes,
    held_in,
    readin_weight,
    qkv_weight,
    out_weight,
    up_weight,
    down_weight,
    norm_gain,
    mlp_gain,
    final_gain,
    readout_weight,
    readout_bias,
):
    frames_all = spikes.shape[0]
    rows_here = frames_all // lax.axis_size("neur")
    masked = (spikes * held_in[None, :]).astype(jnp.bfloat16)
    heldout = (1 - held_in).astype(jnp.float32)
    counts = jnp.sum(spikes, 0).astype(jnp.float32)
    partial_sum = jnp.dot(masked, readin_weight, preferred_element_type=jnp.float32)
    summed = lax.psum(partial_sum, ("neur", "tm"))
    stream = lax.dynamic_slice_in_dim(summed, lax.axis_index("neur") * rows_here, rows_here, 0)
    model_dim = stream.shape[1]
    head_cols = qkv_weight.shape[2]
    local_heads = head_cols // HEAD_DIM
    attn_in = normed(stream, norm_gain).astype(jnp.bfloat16)
    projected = jnp.dot(
        attn_in, qkv_weight.reshape(model_dim, 3 * head_cols), preferred_element_type=jnp.float32
    ).astype(jnp.bfloat16)
    queries = projected[:, :head_cols].reshape(rows_here, local_heads, HEAD_DIM)
    keys_local = projected[:, head_cols : 2 * head_cols]
    values_local = projected[:, 2 * head_cols :]
    scaling = 1.0 / math.sqrt(HEAD_DIM)
    key_rows = lax.all_gather(keys_local, "neur", axis=0, tiled=True).reshape(
        -1, local_heads, HEAD_DIM
    )
    value_rows = lax.all_gather(values_local, "neur", axis=0, tiled=True).reshape(
        -1, local_heads, HEAD_DIM
    )
    scores = (
        jnp.einsum("qhd,khd->hqk", queries, key_rows, preferred_element_type=jnp.float32) * scaling
    )
    weights = jnp.exp(scores)
    numerator = jnp.einsum(
        "hqk,khd->qhd", weights.astype(jnp.bfloat16), value_rows, preferred_element_type=jnp.float32
    )
    denominator = jnp.sum(weights, -1).T
    numerator, denominator = (numerator, denominator)
    heads_out = (
        (numerator / denominator[:, :, None]).astype(jnp.bfloat16).reshape(rows_here, head_cols)
    )
    attn_part = jnp.dot(heads_out, out_weight, preferred_element_type=jnp.float32)
    mixed_state = stream + lax.psum(attn_part, "tm")
    mlp_in = normed(mixed_state, mlp_gain).astype(jnp.bfloat16)
    hidden_act = jax.nn.gelu(jnp.dot(mlp_in, up_weight, preferred_element_type=jnp.float32)).astype(
        jnp.bfloat16
    )
    mlp_part = jnp.dot(hidden_act, down_weight, preferred_element_type=jnp.float32)
    final_state = mixed_state + lax.psum(mlp_part, "tm")
    latents = normed(final_state, final_gain).astype(jnp.bfloat16)
    log_rate = (
        lax.dot_general(
            lax.all_gather(latents, "neur", axis=0, tiled=True),
            readout_weight,
            (((1,), (1,)), ((), ())),
            preferred_element_type=jnp.float32,
        )
        + readout_bias[None, :]
    )
    observed = spikes.astype(jnp.float32)
    model_ll = jnp.sum(observed * log_rate - jnp.exp(log_rate), 0)
    null_ll = counts * jnp.log((counts + 1.0) / frames_all) - (counts + 1.0)
    gained = heldout * (model_ll - null_ll)
    neuron_bits = gained / (math.log(2.0) * (counts + 1.0))
    score_sum, spike_sum = lax.psum((jnp.sum(gained), jnp.sum(heldout * counts)), ("neur", "tm"))
    bits_total = score_sum / (math.log(2.0) * (1.0 + spike_sum))
    return (latents, neuron_bits, bits_total)


def solution(mesh):
    in_specs = (
        P(None, ("neur", "tm")),
        P(("neur", "tm")),
        P(("neur", "tm"), None),
        P(None, None, "tm"),
        P("tm", None),
        P(None, "tm"),
        P("tm", None),
        P(),
        P(),
        P(),
        P(("neur", "tm"), None),
        P(("neur", "tm")),
    )
    out_specs = (P("neur", None), P(("neur", "tm")), P())
    return jax.shard_map(
        on_device, mesh=mesh, in_specs=in_specs, out_specs=out_specs, check_vma=False
    )
```

profile of v0, /device:TPU:1, one launch (start us, length us, event | category | flops | bytes accessed | tf_op | source)
XLA Modules:
  0.0 675.9 jit_solution(17022954513759164385)
XLA Ops:
  7.2 0.0 copy-start
  7.2 0.0 all-reduce.5.cloned.1.call-start
  7.2 1.5 copy-done
  8.8 6.5 fusion
  15.3 0.0 all-reduce.5.cloned.1.call-update
  15.3 0.0 copy-start.3
  15.3 0.0 all-reduce.7.cloned.1.call-start
  15.4 1.4 copy.15
  16.8 269.4 %all-reduce.5.cloned.1.call-done = f32[1024,1024]{1,0:T(8,128)} async-done(((f32[1024,1024]{1,0:T(8,128)}), f32[1024,1024]{1,0:T(8,128)}) %all-reduce.5.cloned.1.call-update) | async-done | bytes 4194320 | tf_op jit(solution)/shard_map/psum | solution.py:34
  286.2 1.0 multiply_reduce_fusion.2
  287.2 1.2 convolution_convert_fusion
  288.5 42.8 %all_gather.10 = bf16[1024,128]{1,0:T(8,128)(2,1)S(1)} all-gather(bf16[32,128]{1,0:T(8,128)(2,1)S(1)} %get-tuple-element.11), channel_id=1, replica_groups=mesh['neur'=32,'tm'=8] {'neur'}, dimensions={0}, use_global_device_ids=true | all-gather | bytes 270336 | tf_op jit(solution)/shard_map/all_gather | solution.py:47
  331.3 0.3 fusion.38
  331.6 42.1 %all_gather.9 = bf16[1024,128]{1,0:T(8,128)(2,1)S(1)} all-gather(bf16[32,128]{1,0:T(8,128)(2,1)S(1)} %get-tuple-element.12), channel_id=1, replica_groups=mesh['neur'=32,'tm'=8] {'neur'}, dimensions={0}, use_global_device_ids=true | all-gather | bytes 270336 | tf_op jit(solution)/shard_map/all_gather | solution.py:50
  373.7 0.0 copy-done.1
  373.7 0.9 fusion.6
  374.6 0.0 all-reduce.7.cloned.1.call-update
  374.6 0.0 all-reduce.9.cloned.1.call-start
  374.7 67.4 %all-reduce.7.cloned.1.call-done = f32[32,1024]{1,0:T(8,128)} async-done(((f32[32,1024]{1,0:T(8,128)}), f32[32,1024]{1,0:T(8,128)}) %all-reduce.7.cloned.1.call-update) | async-done | bytes 131088 | tf_op jit(solution)/shard_map/psum | solution.py:66
  442.1 1.1 multiply_reduce_fusion.1
  443.2 2.8 fusion.16
  446.0 0.0 all-reduce.9.cloned.1.call-update
  446.0 0.0 all-gather.2.cloned.1.call-start
  446.1 76.6 %all-reduce.9.cloned.1.call-done = f32[32,1024]{1,0:T(8,128)} async-done(((f32[32,1024]{1,0:T(8,128)}), f32[32,1024]{1,0:T(8,128)}) %all-reduce.9.cloned.1.call-update) | async-done | bytes 131088 | tf_op jit(solution)/shard_map/psum | solution.py:72
  522.6 1.0 multiply_reduce_fusion
  523.7 0.7 multiply_convert_fusion.2
  524.4 0.0 all-gather.2.cloned.1.call-update
  524.4 2.5 reduce_sum.77
  526.9 58.2 %all-gather.2.cloned.1.call-done = bf16[1024,1024]{1,0:T(8,128)(2,1)} async-done(((bf16[32,1024]{1,0:T(8,128)(2,1)}), bf16[1024,1024]{1,0:T(8,128)(2,1)}) %all-gather.2.cloned.1.call-update) | async-done | bytes 2097168 | tf_op jit(solution)/shard_map/all_gather | solution.py:76
  585.1 6.2 subtract_reduce_fusion
  591.3 1.3 multiply_reduce_fusion.3
  592.6 74.4 %all-reduce = (f32[]{:T(128)}, f32[]{:T(128)}) all-reduce(f32[]{:T(128)} %get-tuple-element.4, f32[]{:T(128)} %get-tuple-element.3), channel_id=1, replica_groups=mesh['neur'=32,'tm'=8] {'neur','tm'}, use_global_device_ids=true, to_apply=%region_10.0 | all-reduce | flops 2 | bytes 16 | tf_op jit(solution)/shard_map/psum | solution.py:88
  (14 shorter events, 0.1 us)
Async XLA Ops:
  7.2 1.6 copy-start
  7.2 279.0 %all-reduce.5.cloned.1.call-start = ((), (), s32[]{:S(2)}) async-start(), calls=%async_computation | async-start | bytes 8388608 | tf_op jit(solution)/shard_map/psum | solution.py:34
  15.3 271.9 %copy-start.2 = (f32[1024]{0:T(1024)S(1)}, f32[1024]{0:T(1024)}, u32[]{:S(2)}) copy-start(f32[1024]{0:T(1024)} %param.19) | copy-start | bytes 12292
  15.3 358.4 %copy-start.1 = (bf16[128,1024]{1,0:T(8,128)(2,1)S(1)}, bf16[128,1024]{1,0:T(8,128)(2,1)}, u32[]{:S(2)}) copy-start(bf16[128,1024]{1,0:T(8,128)(2,1)} %param.16) | copy-start | bytes 786436
  15.3 428.0 %copy-start.5 = (f32[1024]{0:T(1024)S(1)}, f32[1024]{0:T(1024)}, u32[]{:S(2)}) copy-start(f32[1024]{0:T(1024)} %param.20) | copy-start | bytes 12292
  15.3 508.4 %copy-start.3 = (f32[1024]{0:T(1024)S(1)}, f32[1024]{0:T(1024)}, u32[]{:S(2)}) copy-start(f32[1024]{0:T(1024)} %param.21) | copy-start | bytes 12292
  15.3 426.8 %all-reduce.7.cloned.1.call-start = ((), (), s32[]{:S(2)}) async-start(), calls=%async_computation.1 | async-start | bytes 262144 | tf_op jit(solution)/shard_map/psum | solution.py:66
  373.7 211.5 %copy-start.6 = (f32[1024]{0:T(1024)S(1)}, f32[1024]{0:T(1024)}, u32[]{:S(2)}) copy-start(f32[1024]{0:T(1024)} %param.23) | copy-start | bytes 12292
  374.6 148.0 %all-reduce.9.cloned.1.call-start = ((), (), s32[]{:S(2)}) async-start(), calls=%async_computation.2 | async-start | bytes 262144 | tf_op jit(solution)/shard_map/psum | solution.py:72
  446.0 139.1 %all-gather.2.cloned.1.call-start = ((), (), s32[]{:S(2)}) async-start(), calls=%async_computation.3 | async-start | bytes 2162688 | tf_op jit(solution)/shard_map/all_gather | solution.py:76
  526.9 64.4 %copy-start.4 = (s32[1024]{0:T(1024)S(1)}, s32[1024]{0:T(1024)}, u32[]{:S(2)}) copy-start(s32[1024]{0:T(1024)} %param.13) | copy-start | bytes 12292
Sparse Core Ops, SparseCore 0:
  15.4 270.7 all-reduce.4
  374.8 67.3 all-reduce.6
  446.2 76.4 all-reduce.8
  526.0 59.1 all-gather.1
where the time goes:
time: 676 us
  waiting for transfers between devices  472 us (70%)
  blocking collectives  159 us (24%)
  matrix products  18 us (3%)
  between operations  16.2 us (2%)
  other arithmetic  7.64 us (1%)
    psum x1, waiting for transfers between devices, on_device(): summed = lax.psum(partial_sum, ('neur', 'tm'))  269 us
    psum x1, waiting for transfers between devices, on_device(): final_state = mixed_state + lax.psum(mlp_part, 'tm')  76.6 us
    psum x1, blocking collectives, on_device(): lax.psum((jnp.sum(gained), jnp.sum(heldout * counts)), ('neur', 'tm'))  74.4 us
    psum x1, waiting for transfers between devices, on_device(): mixed_state = stream + lax.psum(attn_part, 'tm')  67.4 us
    all_gather x1, waiting for transfers between devices, on_device(): lax.all_gather(latents, 'neur', axis=0, tiled=True)  58.2 us
    all_gather x1, blocking collectives, on_device(): lax.all_gather(keys_local, 'neur', axis=0, tiled=True)  42.8 us
    all_gather x1, blocking collectives, on_device(): lax.all_gather(values_local, 'neur', axis=0, tiled=True)  42.1 us
  transfers between devices with their start and end apart: 4, of which 4 were waited for; matrix products, arithmetic and copies ran while one was open for 1% of the time, Pallas kernels for 0%

commit v1 on v0

--- a/solution.py
+++ b/solution.py
@@ -31,7 +31,7 @@
     heldout = (1 - held_in).astype(jnp.float32)
     counts = jnp.sum(spikes, 0).astype(jnp.float32)
     partial_sum = jnp.dot(masked, readin_weight, preferred_element_type=jnp.float32)
-    summed = lax.psum(partial_sum, ("neur", "tm"))
+    summed = lax.psum(lax.psum(partial_sum, axis_name="neur"), axis_name="tm")
     stream = lax.dynamic_slice_in_dim(summed, lax.axis_index("neur") * rows_here, rows_here, 0)
     model_dim = stream.shape[1]
     head_cols = qkv_weight.shape[2]

time: 676 us -> 899 us (1.33)
  waiting for transfers between devices: 472 us -> 694 us
    psum x1 -> x2, waiting for transfers between devices: 269 us -> 491 us  [on_device(): summed = lax.psum(lax.psum(partial_sum, axis_name='neur'), axis_name='tm')]
  transfers between devices with their start and end apart: 4 -> 5, of which waited for: 4 -> 5; matrix products, arithmetic and copies ran while one was open for 1% -> 0% of each run, Pallas kernels for 0% -> 0%
where the time goes in v1:
time: 899 us
  waiting for transfers between devices  694 us (77%)
  blocking collectives  160 us (18%)
  matrix products  17.9 us (2%)
  between operations  16.2 us (2%)
    psum x2, waiting for transfers between devices, on_device(): summed = lax.psum(lax.psum(partial_sum, axis_name='neur'), axis_name='tm')  491 us
    psum x1, waiting for transfers between devices, on_device(): final_state = mixed_state + lax.psum(mlp_part, 'tm')  76.6 us
    psum x1, blocking collectives, on_device(): lax.psum((jnp.sum(gained), jnp.sum(heldout * counts)), ('neur', 'tm'))  74.3 us
    psum x1, waiting for transfers between devices, on_device(): mixed_state = stream + lax.psum(attn_part, 'tm')  68.4 us
    all_gather x1, waiting for transfers between devices, on_device(): lax.all_gather(latents, 'neur', axis=0, tiled=True)  57.9 us
    all_gather x1, blocking collectives, on_device(): lax.all_gather(keys_local, 'neur', axis=0, tiled=True)  45.7 us
    all_gather x1, blocking collectives, on_device(): lax.all_gather(values_local, 'neur', axis=0, tiled=True)  39.9 us
  transfers between devices with their start and end apart: 5, of which 5 were waited for; matrix products, arithmetic and copies ran while one was open for 0% of the time, Pallas kernels for 0%

profile of v1, /device:TPU:1, one launch (start us, length us, event | category | flops | bytes accessed | tf_op | source)
XLA Modules:
  0.0 898.8 jit_solution(16339645389753368060)
XLA Ops:
  7.2 0.0 all-reduce.6.cloned.1.call-start
  7.2 1.5 copy-done
  8.8 6.4 fusion
  15.2 0.0 all-reduce.6.cloned.1.call-update
  15.2 0.0 all-reduce.8.cloned.1.call-start
  15.3 302.8 %all-reduce.6.cloned.1.call-done = f32[1024,1024]{1,0:T(8,128)} async-done(((f32[1024,1024]{1,0:T(8,128)}), f32[1024,1024]{1,0:T(8,128)}) %all-reduce.6.cloned.1.call-update) | async-done | bytes 4194320 | tf_op jit(solution)/shard_map/psum | solution.py:34
  318.1 0.0 all-reduce.8.cloned.1.call-update
  318.1 0.0 all-reduce.10.cloned.1.call-start
  318.2 1.4 copy.15
  319.6 188.2 %all-reduce.8.cloned.1.call-done = f32[1024,1024]{1,0:T(8,128)} async-done(((f32[1024,1024]{1,0:T(8,128)}), f32[1024,1024]{1,0:T(8,128)}) %all-reduce.8.cloned.1.call-update) | async-done | bytes 4194320 | tf_op jit(solution)/shard_map/psum | solution.py:34
  507.8 1.0 multiply_reduce_fusion.2
  508.8 1.2 convolution_convert_fusion
  510.1 45.7 %all_gather.10 = bf16[1024,128]{1,0:T(8,128)(2,1)S(1)} all-gather(bf16[32,128]{1,0:T(8,128)(2,1)S(1)} %get-tuple-element.11), channel_id=1, replica_groups=mesh['neur'=32,'tm'=8] {'neur'}, dimensions={0}, use_global_device_ids=true | all-gather | bytes 270336 | tf_op jit(solution)/shard_map/all_gather | solution.py:47
  555.7 0.3 fusion.38
  556.0 39.9 %all_gather.9 = bf16[1024,128]{1,0:T(8,128)(2,1)S(1)} all-gather(bf16[32,128]{1,0:T(8,128)(2,1)S(1)} %get-tuple-element.12), channel_id=1, replica_groups=mesh['neur'=32,'tm'=8] {'neur'}, dimensions={0}, use_global_device_ids=true | all-gather | bytes 270336 | tf_op jit(solution)/shard_map/all_gather | solution.py:50
  595.9 0.9 fusion.6
  596.9 0.0 all-reduce.10.cloned.1.call-update
  596.9 0.0 all-reduce.12.cloned.1.call-start
  597.0 68.4 %all-reduce.10.cloned.1.call-done = f32[32,1024]{1,0:T(8,128)} async-done(((f32[32,1024]{1,0:T(8,128)}), f32[32,1024]{1,0:T(8,128)}) %all-reduce.10.cloned.1.call-update) | async-done | bytes 131088 | tf_op jit(solution)/shard_map/psum | solution.py:66
  665.4 1.1 multiply_reduce_fusion.1
  666.5 2.8 fusion.16
  669.3 0.0 all-reduce.12.cloned.1.call-update
  669.3 0.0 all-gather.2.cloned.1.call-start
  669.4 76.6 %all-reduce.12.cloned.1.call-done = f32[32,1024]{1,0:T(8,128)} async-done(((f32[32,1024]{1,0:T(8,128)}), f32[32,1024]{1,0:T(8,128)}) %all-reduce.12.cloned.1.call-update) | async-done | bytes 131088 | tf_op jit(solution)/shard_map/psum | solution.py:72
  745.9 1.0 multiply_reduce_fusion
  747.0 0.7 multiply_convert_fusion.2
  747.7 0.0 all-gather.2.cloned.1.call-update
  747.7 2.5 reduce_sum.77
  750.2 57.9 %all-gather.2.cloned.1.call-done = bf16[1024,1024]{1,0:T(8,128)(2,1)} async-done(((bf16[32,1024]{1,0:T(8,128)(2,1)}), bf16[1024,1024]{1,0:T(8,128)(2,1)}) %all-gather.2.cloned.1.call-update) | async-done | bytes 2097168 | tf_op jit(solution)/shard_map/all_gather | solution.py:76
  808.1 6.2 subtract_reduce_fusion
  814.3 1.3 multiply_reduce_fusion.3
  815.6 74.3 %all-reduce = (f32[]{:T(128)}, f32[]{:T(128)}) all-reduce(f32[]{:T(128)} %get-tuple-element.4, f32[]{:T(128)} %get-tuple-element.3), channel_id=1, replica_groups=mesh['neur'=32,'tm'=8] {'neur','tm'}, use_global_device_ids=true, to_apply=%region_11.0 | all-reduce | flops 2 | bytes 16 | tf_op jit(solution)/shard_map/psum | solution.py:88
  (17 shorter events, 0.1 us)
Async XLA Ops:
  7.2 1.6 copy-start
  7.2 310.9 %all-reduce.6.cloned.1.call-start = ((), (), s32[]{:S(2)}) async-start(), calls=%async_computation | async-start | bytes 8388608 | tf_op jit(solution)/shard_map/psum | solution.py:34
  15.2 493.6 %copy-start.2 = (f32[1024]{0:T(1024)S(1)}, f32[1024]{0:T(1024)}, u32[]{:S(2)}) copy-start(f32[1024]{0:T(1024)} %param.19) | copy-start | bytes 12292
  15.2 580.7 %copy-start.1 = (bf16[128,1024]{1,0:T(8,128)(2,1)S(1)}, bf16[128,1024]{1,0:T(8,128)(2,1)}, u32[]{:S(2)}) copy-start(bf16[128,1024]{1,0:T(8,128)(2,1)} %param.16) | copy-start | bytes 786436
  15.2 492.5 %all-reduce.8.cloned.1.call-start = ((), (), s32[]{:S(2)}) async-start(), calls=%async_computation.1 | async-start | bytes 8388608 | tf_op jit(solution)/shard_map/psum | solution.py:34
  318.1 348.4 %copy-start.5 = (f32[1024]{0:T(1024)S(1)}, f32[1024]{0:T(1024)}, u32[]{:S(2)}) copy-start(f32[1024]{0:T(1024)} %param.20) | copy-start | bytes 12292
  318.1 428.9 %copy-start.3 = (f32[1024]{0:T(1024)S(1)}, f32[1024]{0:T(1024)}, u32[]{:S(2)}) copy-start(f32[1024]{0:T(1024)} %param.21) | copy-start | bytes 12292
  318.1 347.3 %all-reduce.10.cloned.1.call-start = ((), (), s32[]{:S(2)}) async-start(), calls=%async_computation.2 | async-start | bytes 262144 | tf_op jit(solution)/shard_map/psum | solution.py:66
  595.9 212.1 %copy-start.6 = (f32[1024]{0:T(1024)S(1)}, f32[1024]{0:T(1024)}, u32[]{:S(2)}) copy-start(f32[1024]{0:T(1024)} %param.23) | copy-start | bytes 12292
  596.9 149.0 %all-reduce.12.cloned.1.call-start = ((), (), s32[]{:S(2)}) async-start(), calls=%async_computation.3 | async-start | bytes 262144 | tf_op jit(solution)/shard_map/psum | solution.py:72
  669.3 138.8 %all-gather.2.cloned.1.call-start = ((), (), s32[]{:S(2)}) async-start(), calls=%async_computation.4 | async-start | bytes 2162688 | tf_op jit(solution)/shard_map/all_gather | solution.py:76
  750.2 64.1 %copy-start.4 = (s32[1024]{0:T(1024)S(1)}, s32[1024]{0:T(1024)}, u32[]{:S(2)}) copy-start(s32[1024]{0:T(1024)} %param.13) | copy-start | bytes 12292
Sparse Core Ops, SparseCore 0:
  15.4 302.6 all-reduce.5
  320.7 186.9 all-reduce.7
  597.0 68.2 all-reduce.9
  669.4 76.4 all-reduce.11
  748.9 59.1 all-gather.1
